TPU v7x, 32 devices: a whole 2x2x4 slice. The times are simulated.
32 devices in a mesh: win: 8 (over z, x), atom: 4 (over y, core).
Axes of the slice: x: 2, y: 2, z: 4, core: 2. Of those that a mesh axis runs over, the one named last changes fastest.
Arguments:
- retarded: bfloat16 [64, 8, 2, 128, 128], P(('win', 'atom')), may hold values from -0.375 to 0.375
- sigma_in: bfloat16 [64, 8, 2, 128, 128], P(('win', 'atom')), may hold values from -6 to 6
- bit_shifts: int32 [3], replicated, may hold values from 0 to 2, as said below
- occupation: float32 [3], replicated, may hold values from 0.3 to 3
- neighbors: int32 [8, 3], replicated, may hold values from 0 to 7, as said below
- coupling: bfloat16 [3, 128, 128], replicated, may hold values from -0.375 to 0.375
Outputs:
- self_energy: bfloat16 [64, 8, 2, 128, 128], P('win', 'atom')
Inputs may be any that keep to these rules, and one draw needn't show every extreme that they name: `bit_shifts`: three different values; among them are 0 and 2, in an order drawn afresh. `neighbors`: column 0 of row b is b itself; the other columns of row b lie within b - 1 to b + 1.
All inputs are finite; a program needn't handle non-finite values.
Results may differ from a plain program's by a relative error of at most 0.007.
Values may be sent and summed in bfloat16 or wider, within the bound.
No kernel may reach another device: no remote copies, remote signals or barrier semaphores. Data moves between devices by JAX's collectives and lax.ppermute only.
A program may use at most 128 MiB of HBM per device.

v0:
```python
import jax
import jax.numpy as jnp
from jax import lax
from jax.sharding import PartitionSpec as P


def partner(value, axis, distance):
    mask = 2**distance
    pairs = [(source, source ^ mask) for source in range(lax.axis_size(axis))]
    return lax.ppermute(value, axis, pairs)


def complex_product(left, right, form):
    real_part = jnp.einsum(
        form, left[:, :, 0], right[:, :, 0], preferred_element_type=jnp.float32
    ) - jnp.einsum(form, left[:, :, 1], right[:, :, 1], preferred_element_type=jnp.float32)
    imag_part = jnp.einsum(
        form, left[:, :, 0], right[:, :, 1], preferred_element_type=jnp.float32
    ) + jnp.einsum(form, left[:, :, 1], right[:, :, 0], preferred_element_type=jnp.float32)
    return jnp.stack([real_part, imag_part], axis=2).astype(jnp.bfloat16)


def partner_sum(lesser, bit_shifts, occupation):
    bit_count = lax.axis_size("win").bit_length() - 1
    summed = jnp.zeros(lesser.shape, jnp.float32)
    for bit_number in range(bit_count):
        weight = jnp.sum(jnp.where(bit_shifts == bit_number, occupation, 0.0))
        arrived = partner(lesser, "win", bit_number)
        summed = summed + weight * arrived.astype(jnp.float32)
    return summed.astype(jnp.bfloat16)


def couple(source, indices, coupling):
    directions = coupling.shape[0]
    picks = [jnp.take(source, indices[:, direction], axis=1) for direction in range(directions)]
    result = jnp.zeros(picks[0].shape, jnp.float32)
    for direction in range(directions):
        bent = jnp.einsum(
            "ij,erxjk->erxik",
            coupling[direction],
            picks[direction],
            preferred_element_type=jnp.float32,
        ).astype(jnp.bfloat16)
        result = result + jnp.einsum(
            "erxij,kj->erxik", bent, coupling[direction], preferred_element_type=jnp.float32
        )
    return result.astype(jnp.bfloat16)


def on_device(retarded, sigma_in, bit_shifts, occupation, neighbors, coupling):
    product = complex_product(retarded, sigma_in, "ebij,ebjk->ebik")
    lesser = complex_product(product, retarded, "ebij,ebkj->ebik")
    partners = partner_sum(lesser, bit_shifts, occupation)
    energy_side = couple(partners, neighbors, coupling)
    return lax.all_to_all(energy_side, "atom", split_axis=1, concat_axis=0, tiled=True)


def solution(mesh):
    return jax.shard_map(
        on_device,
        mesh=mesh,
        in_specs=(
            P(("win", "atom"), None, None, None, None),
            P(("win", "atom"), None, None, None, None),
            P(),
            P(),
            P(),
            P(),
        ),
        out_specs=P("win", "atom", None, None, None),
        check_vma=False,
    )
```

profile of v0, /device:TPU:0, one launch (start us, length us, event | category | flops | bytes accessed | tf_op | source)
XLA Modules:
  0.0 89.7 jit_solution(15645201465588671409)
XLA Ops:
  0.0 1.6 %fusion.17 = f32[2,8,128,128]{3,2,1,0:T(8,128)S(1)} fusion(bf16[2,8,2,128,128]{4,3,2,1,0:T(8,128)(2,1)} %param.9, bf16[2,8,2,128,128]{4,3,2,1,0:T(8,128)(2,1)} %param.8), kind=kOutput, calls=%fused_computation.30 | convolution fusion | flops 67108864 | bytes 2097152 | tf_op jit(solution)/shard_map/ebij,ebjk->ebik/dot_general | solution.py:17
  1.7 0.0 copy-done
  1.7 0.2 copy-done.1
  1.9 0.3 fusion.26
  2.2 0.3 fusion.5
  2.5 0.5 fusion.20
  2.9 0.5 fusion.30
  3.4 0.3 fusion.6
  3.7 0.5 fusion.9
  4.2 0.0 copy-start.3
  4.2 0.0 copy-start.4
  4.2 0.0 copy-start.5
  4.3 0.5 fusion.10
  4.7 0.1 pad_maximum_fusion
  4.8 4.1 %collective-permute-start.2 = (bf16[2,8,2,128,128]{4,3,1,0,2:T(8,128)(2,1)S(1)}, bf16[2,8,2,128,128]{4,3,1,0,2:T(8,128)(2,1)S(1)}, u32[]{:S(2)}, u32[]{:S(2)}) collective-permute-start(bf16[2,8,2,128,128]{4,3,1,0,2:T(8,128)(2,1)S(1)} %pad_maximum_fusion), channel_id=1, source_target_pairs={{0,16},{4,20},{8,24},{12,28},{16,0},{20,4},{24,8},{28,12},{1,17},{... | collective-permute-start | bytes 3145736 | tf_op jit(solution)/shard_map/ppermute | solution.py:10
  9.0 1.6 %collective-permute-start.1 = (bf16[2,8,2,128,128]{4,3,1,0,2:T(8,128)(2,1)S(1)}, bf16[2,8,2,128,128]{4,3,1,0,2:T(8,128)(2,1)S(1)}, u32[]{:S(2)}, u32[]{:S(2)}) collective-permute-start(bf16[2,8,2,128,128]{4,3,1,0,2:T(8,128)(2,1)S(1)} %pad_maximum_fusion), channel_id=1, source_target_pairs={{0,8},{4,12},{8,0},{12,4},{16,24},{20,28},{24,16},{28,20},{1,9},{5... | collective-permute-start | bytes 3145736 | tf_op jit(solution)/shard_map/ppermute | solution.py:10
  10.5 1.5 %collective-permute-start = (bf16[2,8,2,128,128]{4,3,1,0,2:T(8,128)(2,1)S(1)}, bf16[2,8,2,128,128]{4,3,1,0,2:T(8,128)(2,1)S(1)}, u32[]{:S(2)}, u32[]{:S(2)}) collective-permute-start(bf16[2,8,2,128,128]{4,3,1,0,2:T(8,128)(2,1)S(1)} %pad_maximum_fusion), channel_id=1, source_target_pairs={{0,4},{4,0},{8,12},{12,8},{16,20},{20,16},{24,28},{28,24},{1,5},{5... | collective-permute-start | bytes 3145736 | tf_op jit(solution)/shard_map/ppermute | solution.py:10
  12.1 0.6 fusion.57
  12.8 41.9 %collective-permute-done.2 = bf16[2,8,2,128,128]{4,3,1,0,2:T(8,128)(2,1)S(1)} collective-permute-done((bf16[2,8,2,128,128]{4,3,1,0,2:T(8,128)(2,1)S(1)}, bf16[2,8,2,128,128]{4,3,1,0,2:T(8,128)(2,1)S(1)}, u32[]{:S(2)}, u32[]{:S(2)}) %collective-permute-start.2) | collective-permute-done | bytes 1048608 | tf_op jit(solution)/shard_map/ppermute | solution.py:10
  54.7 0.2 collective-permute-done.1
  54.9 0.0 collective-permute-done
  54.9 2.5 %add_convert_fusion.1 = bf16[2,8,2,128,128]{4,3,1,0,2:T(8,128)(2,1)S(1)} fusion(bf16[2,8,2,128,128]{4,3,1,0,2:T(8,128)(2,1)S(1)} %collective-permute-done.2, bf16[2,8,2,128,128]{4,3,1,0,2:T(8,128)(2,1)S(1)} %collective-permute-done.1, bf16[2,8,2,128,128]{4,3,1,0,2:T(8,128)(2,1)S(1)} %collective-permute-done, f32[]{:T(128)} %get-tuple-element.7, ...), kind=kLoop, calls=%fused_computation.4 | loop fusion | flops 4718592 | bytes 4194316 | tf_op jit(solution)/shard_map/convert_element_type | solution.py:30
  57.4 0.7 gather_fusion.2
  58.1 0.7 gather_fusion.1
  58.9 1.7 %gather_fusion = bf16[8,2,2,128,128]{4,3,1,2,0:T(8,128)(2,1)} fusion(bf16[2,8,2,128,128]{4,3,1,0,2:T(8,128)(2,1)S(1)} %add_convert_fusion.1, s32[1024]{0:T(1024)S(1)} %pad_clamp_fusion.2), kind=kCustom, calls=%fused_computation.clone | custom fusion | bytes 2097184 | tf_op jit(solution)/shard_map/jit(_take)/gather | solution.py:35
  60.6 1.2 %select_bitcast_fusion = (bf16[2,8,2,128,128]{4,3,0,2,1:T(8,128)(2,1)S(1)}, bf16[2,8,2,128,128]{4,3,0,2,1:T(8,128)(2,1)}) fusion(bf16[8,2,2,128,128]{4,3,1,2,0:T(8,128)(2,1)S(1)} %gather_fusion.2, pred[8]{0:T(512)(128)(4,1)S(1)} %get-tuple-element.9, bf16[8,2,2,128,128]{4,3,1,2,0:T(8,128)(2,1)S(1)} %gather_fusion.1, pred[8]{0:T(512)(128)(4,1)S(1)} %get-tuple-element.17), kind=kLoop, calls=%fused_computation.27 | loop fusion | flops 1048576 | bytes 4194320 | tf_op jit(solution)/shard_map/jit(_take)/select_n | solution.py:35
  61.8 1.9 %fusion.3 = f32[2,8,2,128,128]{4,3,2,1,0:T(8,128)S(1)} fusion(bf16[2,8,2,128,128]{4,3,0,2,1:T(8,128)(2,1)} %get-tuple-element.20, bf16[3,128,128]{2,1,0:T(8,128)(2,1)S(1)} %copy-done.2), kind=kOutput, calls=%fused_computation.11 | convolution fusion | flops 268959744 | bytes 3211264 | tf_op jit(solution)/shard_map/erxij,kj->erxik/dot_general | solution.py:44
  63.7 3.3 %fusion.1 = f32[2,8,2,128,128]{4,3,2,1,0:T(8,128)} fusion(bf16[3,128,128]{2,1,0:T(8,128)(2,1)S(1)} %copy-done.2, bf16[8,2,2,128,128]{4,3,1,2,0:T(8,128)(2,1)} %gather_fusion, pred[8]{0:T(512)(128)(4,1)S(1)} %get-tuple-element.15), kind=kOutput, calls=%fused_computation.9 | convolution fusion | flops 269484032 | bytes 3211776 | tf_op jit(solution)/shard_map/erxij,kj->erxik/dot_general | solution.py:44
  67.0 3.3 %add_convert_fusion = bf16[2,8,2,128,128]{4,3,2,1,0:T(8,128)(2,1)} fusion(f32[2,8,2,128,128]{4,3,2,1,0:T(8,128)} %fusion.1, f32[2,8,2,128,128]{4,3,2,1,0:T(8,128)S(1)} %fusion.3, bf16[2,8,2,128,128]{4,3,0,2,1:T(8,128)(2,1)S(1)} %get-tuple-element.19, bf16[3,128,128]{2,1,0:T(8,128)(2,1)S(1)} %copy-done.2), kind=kOutput, calls=%fused_computation.3 | convolution fusion | flops 270532608 | bytes 6356992 | tf_op jit(solution)/shard_map/erxij,kj->erxik/dot_general | solution.py:44
  70.3 1.3 %copy.16 = bf16[2,8,2,128,128]{4,3,2,0,1:T(8,128)(2,1)S(1)} copy(bf16[2,8,2,128,128]{4,3,2,1,0:T(8,128)(2,1)} %add_convert_fusion) | data formatting | bytes 2097152 | tf_op jit(solution)/shard_map/convert_element_type | solution.py:47
  71.6 17.1 %all_to_all.18 = bf16[2,8,2,128,128]{4,3,2,0,1:T(8,128)(2,1)S(1)} all-to-all(bf16[2,8,2,128,128]{4,3,2,0,1:T(8,128)(2,1)S(1)} %copy.16), channel_id=1, replica_groups=mesh['win'=8,'atom'=4] {'atom'}, dimensions={1} | all-to-all | bytes 2097152 | tf_op jit(solution)/shard_map/all_to_all | solution.py:55
  88.7 1.0 %copy.17 = bf16[4,2,2,2,128,128]{5,4,3,2,1,0:T(8,128)(2,1)} copy(bf16[4,2,2,2,128,128]{5,4,3,1,2,0:T(8,128)(2,1)S(1)} %bitcast.102) | data formatting | bytes 2097152 | tf_op jit(solution)/shard_map/all_to_all | solution.py:55
  (11 shorter events, 0.0 us)
Async XLA Ops:
  0.0 1.7 %copy-start = (bf16[2,8,2,128,128]{4,3,2,1,0:T(8,128)(2,1)S(1)}, bf16[2,8,2,128,128]{4,3,2,1,0:T(8,128)(2,1)}, u32[]{:S(2)}) copy-start(bf16[2,8,2,128,128]{4,3,2,1,0:T(8,128)(2,1)} %param.8) | copy-start | bytes 3145732
  0.0 1.9 %copy-start.1 = (bf16[2,8,2,128,128]{4,3,2,1,0:T(8,128)(2,1)S(1)}, bf16[2,8,2,128,128]{4,3,2,1,0:T(8,128)(2,1)}, u32[]{:S(2)}) copy-start(bf16[2,8,2,128,128]{4,3,2,1,0:T(8,128)(2,1)} %param.9) | copy-start | bytes 3145732
  4.2 7.8 %copy-start.3 = (s32[8,3]{0,1:T(4,128)S(1)}, s32[8,3]{0,1:T(4,128)}, u32[]{:S(2)}) copy-start(s32[8,3]{0,1:T(4,128)} %param.12) | copy-start | bytes 292
  4.2 7.9 %copy-start.4 = (f32[3]{0:T(128)S(1)}, f32[3]{0:T(128)}, u32[]{:S(2)}) copy-start(f32[3]{0:T(128)} %param.11) | copy-start | bytes 40
  4.2 7.9 %copy-start.5 = (s32[3]{0:T(128)S(1)}, s32[3]{0:T(128)}, u32[]{:S(2)}) copy-start(s32[3]{0:T(128)} %param.10) | copy-start | bytes 40
  4.8 49.8 %collective-permute-start.2 = (bf16[2,8,2,128,128]{4,3,1,0,2:T(8,128)(2,1)S(1)}, bf16[2,8,2,128,128]{4,3,1,0,2:T(8,128)(2,1)S(1)}, u32[]{:S(2)}, u32[]{:S(2)}) collective-permute-start(bf16[2,8,2,128,128]{4,3,1,0,2:T(8,128)(2,1)S(1)} %pad_maximum_fusion), channel_id=1, source_target_pairs={{0,16},{4,20},{8,24},{12,28},{16,0},{20,4},{24,8},{28,12},{1,17},{... | collective-permute-start | bytes 3145736 | tf_op jit(solution)/shard_map/ppermute | solution.py:10
  9.0 45.9 %collective-permute-start.1 = (bf16[2,8,2,128,128]{4,3,1,0,2:T(8,128)(2,1)S(1)}, bf16[2,8,2,128,128]{4,3,1,0,2:T(8,128)(2,1)S(1)}, u32[]{:S(2)}, u32[]{:S(2)}) collective-permute-start(bf16[2,8,2,128,128]{4,3,1,0,2:T(8,128)(2,1)S(1)} %pad_maximum_fusion), channel_id=1, source_target_pairs={{0,8},{4,12},{8,0},{12,4},{16,24},{20,28},{24,16},{28,20},{1,9},{5... | collective-permute-start | bytes 3145736 | tf_op jit(solution)/shard_map/ppermute | solution.py:10
  10.5 44.4 %collective-permute-start = (bf16[2,8,2,128,128]{4,3,1,0,2:T(8,128)(2,1)S(1)}, bf16[2,8,2,128,128]{4,3,1,0,2:T(8,128)(2,1)S(1)}, u32[]{:S(2)}, u32[]{:S(2)}) collective-permute-start(bf16[2,8,2,128,128]{4,3,1,0,2:T(8,128)(2,1)S(1)} %pad_maximum_fusion), channel_id=1, source_target_pairs={{0,4},{4,0},{8,12},{12,8},{16,20},{20,16},{24,28},{28,24},{1,5},{5... | collective-permute-start | bytes 3145736 | tf_op jit(solution)/shard_map/ppermute | solution.py:10
  60.5 1.2 %copy-start.2 = (bf16[3,128,128]{2,1,0:T(8,128)(2,1)S(1)}, bf16[3,128,128]{2,1,0:T(8,128)(2,1)}, u32[]{:S(2)}) copy-start(bf16[3,128,128]{2,1,0:T(8,128)(2,1)} %param.13) | copy-start | bytes 294916
where the time goes:
time: 90 us; the launch traced here: 89.7 us
  waiting for transfers between devices  42.1 us (47%)
  blocking collectives  17.1 us (19%)
  matrix products  13 us (14%)
  starting transfers between devices  7.2 us (8%)
  local copies, waits for them, and re-layouts  5.71 us (6%)
  other arithmetic  4.47 us (5%)
    ppermute x3, waiting for transfers between devices, partner(): return lax.ppermute(value, axis, pairs)  42.1 us
    all_to_all x1, blocking collectives, on_device(): lax.all_to_all(energy_side, 'atom', split_axis=1, concat_axis=0, tiled=True)  17.1 us
    dot_general x3, matrix products, couple(): jnp.einsum('erxij,kj->erxik', bent, coupling[direction], preferred_elemen...  8.53 us
    ppermute x3, starting transfers between devices, partner(): return lax.ppermute(value, axis, pairs)  7.2 us
    gather x3, local copies, waits for them, and re-layouts, couple(): jnp.take(source, indices[:, direction], axis=1)  3.15 us
    convert_element_type x1, other arithmetic, partner_sum(): return summed.astype(jnp.bfloat16)  2.49 us
    dot_general x2, matrix products, complex_product(): jnp.einsum(form, left[:, :, 0], right[:, :, 1], preferred_element_type=jn...  2.13 us
  transfers between devices with their start and end apart: 3, of which 2 were waited for; matrix products, arithmetic and copies ran while one was open for 1% of the time, Pallas kernels for 0%

commit v1 on v0

--- a/solution.py
+++ b/solution.py
@@ -52,7 +52,12 @@
     lesser = complex_product(product, retarded, "ebij,ebkj->ebik")
     partners = partner_sum(lesser, bit_shifts, occupation)
     energy_side = couple(partners, neighbors, coupling)
-    return lax.all_to_all(energy_side, "atom", split_axis=1, concat_axis=0, tiled=True)
+    return jnp.concatenate(
+        lax.all_to_all(
+            jnp.stack(jnp.split(energy_side, lax.axis_size("atom"), axis=1)), "atom", 0, 0
+        ),
+        axis=0,
+    )
 
 
 def solution(mesh):

time: 90 us -> 90 us (level)
    convert_element_type x1 -> x0, local copies, waits for them, and re-layouts: 1.29 us -> none  [couple(): return result.astype(jnp.bfloat16)]
    another operation x0 -> x1, local copies, waits for them, and re-layouts: none -> 1.26 us  [on_device(): jnp.stack(jnp.split(energy_side, lax.axis_size('atom'), axis=1))]
    all_to_all x1 -> x0, local copies, waits for them, and re-layouts: 1.04 us -> none  [on_device(): lax.all_to_all(energy_side, 'atom', split_axis=1, concat_axis=0, tiled=True)]
    unnamed x12 -> x13, local copies, waits for them, and re-layouts: 0.23 us -> 1.2 us
where the time goes in v1:
time: 90 us; the launch traced here: 89.7 us
  waiting for transfers between devices  42.2 us (47%)
  blocking collectives  17.1 us (19%)
  matrix products  13 us (14%)
  starting transfers between devices  7.2 us (8%)
  local copies, waits for them, and re-layouts  5.6 us (6%)
  other arithmetic  4.53 us (5%)
    ppermute x3, waiting for transfers between devices, partner(): return lax.ppermute(value, axis, pairs)  42.2 us
    all_to_all x1, blocking collectives, on_device(): lax.all_to_all(jnp.stack(jnp.split(energy_side, lax.axis_size('atom'), ax...  17.1 us
    dot_general x3, matrix products, couple(): jnp.einsum('erxij,kj->erxik', bent, coupling[direction], preferred_elemen...  8.52 us
    ppermute x3, starting transfers between devices, partner(): return lax.ppermute(value, axis, pairs)  7.2 us
    gather x3, local copies, waits for them, and re-layouts, couple(): jnp.take(source, indices[:, direction], axis=1)  3.15 us
    convert_element_type x1, other arithmetic, partner_sum(): return summed.astype(jnp.bfloat16)  2.44 us
    dot_general x2, matrix products, complex_product(): jnp.einsum(form, left[:, :, 0], right[:, :, 1], preferred_element_type=jn...  2.13 us
  transfers between devices with their start and end apart: 3, of which 2 were waited for; matrix products, arithmetic and copies ran while one was open for 1% of the time, Pallas kernels for 0%

profile of v1, /device:TPU:0, one launch (start us, length us, event | category | flops | bytes accessed | tf_op | source)
XLA Modules:
  0.0 89.7 jit_solution(13768394453677847581)
XLA Ops:
  0.0 1.6 %fusion.17 = f32[2,8,128,128]{3,2,1,0:T(8,128)S(1)} fusion(bf16[2,8,2,128,128]{4,3,2,1,0:T(8,128)(2,1)} %param.9, bf16[2,8,2,128,128]{4,3,2,1,0:T(8,128)(2,1)} %param.8), kind=kOutput, calls=%fused_computation.31 | convolution fusion | flops 67108864 | bytes 2097152 | tf_op jit(solution)/shard_map/ebij,ebjk->ebik/dot_general | solution.py:17
  1.7 0.2 copy-done.1
  1.9 0.3 fusion.26
  2.2 0.3 fusion.5
  2.5 0.5 fusion.20
  2.9 0.5 fusion.30
  3.4 0.3 fusion.6
  3.7 0.5 fusion.9
  4.2 0.0 copy-start.3
  4.2 0.0 copy-start.4
  4.2 0.0 copy-start.5
  4.3 0.5 fusion.10
  4.7 0.1 pad_maximum_fusion
  4.8 4.1 %collective-permute-start.2 = (bf16[2,8,2,128,128]{4,3,1,0,2:T(8,128)(2,1)S(1)}, bf16[2,8,2,128,128]{4,3,1,0,2:T(8,128)(2,1)S(1)}, u32[]{:S(2)}, u32[]{:S(2)}) collective-permute-start(bf16[2,8,2,128,128]{4,3,1,0,2:T(8,128)(2,1)S(1)} %pad_maximum_fusion), channel_id=1, source_target_pairs={{0,16},{4,20},{8,24},{12,28},{16,0},{20,4},{24,8},{28,12},{1,17},{... | collective-permute-start | bytes 3145736 | tf_op jit(solution)/shard_map/ppermute | solution.py:10
  9.0 1.6 %collective-permute-start.1 = (bf16[2,8,2,128,128]{4,3,1,0,2:T(8,128)(2,1)S(1)}, bf16[2,8,2,128,128]{4,3,1,0,2:T(8,128)(2,1)S(1)}, u32[]{:S(2)}, u32[]{:S(2)}) collective-permute-start(bf16[2,8,2,128,128]{4,3,1,0,2:T(8,128)(2,1)S(1)} %pad_maximum_fusion), channel_id=1, source_target_pairs={{0,8},{4,12},{8,0},{12,4},{16,24},{20,28},{24,16},{28,20},{1,9},{5... | collective-permute-start | bytes 3145736 | tf_op jit(solution)/shard_map/ppermute | solution.py:10
  10.5 1.5 %collective-permute-start = (bf16[2,8,2,128,128]{4,3,1,0,2:T(8,128)(2,1)S(1)}, bf16[2,8,2,128,128]{4,3,1,0,2:T(8,128)(2,1)S(1)}, u32[]{:S(2)}, u32[]{:S(2)}) collective-permute-start(bf16[2,8,2,128,128]{4,3,1,0,2:T(8,128)(2,1)S(1)} %pad_maximum_fusion), channel_id=1, source_target_pairs={{0,4},{4,0},{8,12},{12,8},{16,20},{20,16},{24,28},{28,24},{1,5},{5... | collective-permute-start | bytes 3145736 | tf_op jit(solution)/shard_map/ppermute | solution.py:10
  12.1 0.6 fusion.57
  12.7 42.0 %collective-permute-done.2 = bf16[2,8,2,128,128]{4,3,1,0,2:T(8,128)(2,1)S(1)} collective-permute-done((bf16[2,8,2,128,128]{4,3,1,0,2:T(8,128)(2,1)S(1)}, bf16[2,8,2,128,128]{4,3,1,0,2:T(8,128)(2,1)S(1)}, u32[]{:S(2)}, u32[]{:S(2)}) %collective-permute-start.2) | collective-permute-done | bytes 1048608 | tf_op jit(solution)/shard_map/ppermute | solution.py:10
  54.7 0.2 collective-permute-done.1
  54.9 0.0 collective-permute-done
  54.9 2.4 %add_convert_fusion.1 = bf16[2,8,2,128,128]{4,3,1,0,2:T(8,128)(2,1)S(1)} fusion(bf16[2,8,2,128,128]{4,3,1,0,2:T(8,128)(2,1)S(1)} %collective-permute-done.2, bf16[2,8,2,128,128]{4,3,1,0,2:T(8,128)(2,1)S(1)} %collective-permute-done.1, bf16[2,8,2,128,128]{4,3,1,0,2:T(8,128)(2,1)S(1)} %collective-permute-done, f32[]{:T(128)} %get-tuple-element.7, ...), kind=kLoop, calls=%fused_computation.4 | loop fusion | flops 4718592 | bytes 4194316 | tf_op jit(solution)/shard_map/convert_element_type | solution.py:30
  57.3 0.7 gather_fusion.2
  58.1 0.7 gather_fusion.1
  58.8 1.7 %gather_fusion = bf16[8,2,2,128,128]{4,3,1,2,0:T(8,128)(2,1)} fusion(bf16[2,8,2,128,128]{4,3,1,0,2:T(8,128)(2,1)S(1)} %add_convert_fusion.1, s32[1024]{0:T(1024)S(1)} %pad_clamp_fusion.2), kind=kCustom, calls=%fused_computation.clone | custom fusion | bytes 2097184 | tf_op jit(solution)/shard_map/jit(_take)/gather | solution.py:35
  60.5 1.2 %select_bitcast_fusion = (bf16[2,8,2,128,128]{4,3,0,2,1:T(8,128)(2,1)S(1)}, bf16[2,8,2,128,128]{4,3,0,2,1:T(8,128)(2,1)}) fusion(bf16[8,2,2,128,128]{4,3,1,2,0:T(8,128)(2,1)S(1)} %gather_fusion.2, pred[8]{0:T(512)(128)(4,1)S(1)} %get-tuple-element.9, bf16[8,2,2,128,128]{4,3,1,2,0:T(8,128)(2,1)S(1)} %gather_fusion.1, pred[8]{0:T(512)(128)(4,1)S(1)} %get-tuple-element.21), kind=kLoop, calls=%fused_computation.28 | loop fusion | flops 1048576 | bytes 4194320 | tf_op jit(solution)/shard_map/jit(_take)/select_n | solution.py:35
  61.7 1.9 %fusion.3 = f32[2,8,2,128,128]{4,3,2,1,0:T(8,128)S(1)} fusion(bf16[2,8,2,128,128]{4,3,0,2,1:T(8,128)(2,1)} %get-tuple-element.24, bf16[3,128,128]{2,1,0:T(8,128)(2,1)S(1)} %copy-done.2), kind=kOutput, calls=%fused_computation.11 | convolution fusion | flops 268959744 | bytes 3211264 | tf_op jit(solution)/shard_map/erxij,kj->erxik/dot_general | solution.py:44
  63.6 3.3 %fusion.1 = f32[2,8,2,128,128]{4,3,2,1,0:T(8,128)} fusion(bf16[3,128,128]{2,1,0:T(8,128)(2,1)S(1)} %copy-done.2, bf16[8,2,2,128,128]{4,3,1,2,0:T(8,128)(2,1)} %gather_fusion, pred[8]{0:T(512)(128)(4,1)S(1)} %get-tuple-element.19), kind=kOutput, calls=%fused_computation.9 | convolution fusion | flops 269484032 | bytes 3211776 | tf_op jit(solution)/shard_map/erxij,kj->erxik/dot_general | solution.py:44
  67.0 3.3 %add_convert_fusion = bf16[2,8,2,128,128]{4,3,2,1,0:T(8,128)(2,1)} fusion(f32[2,8,2,128,128]{4,3,2,1,0:T(8,128)} %fusion.1, f32[2,8,2,128,128]{4,3,2,1,0:T(8,128)S(1)} %fusion.3, bf16[2,8,2,128,128]{4,3,0,2,1:T(8,128)(2,1)S(1)} %get-tuple-element.23, bf16[3,128,128]{2,1,0:T(8,128)(2,1)S(1)} %copy-done.2), kind=kOutput, calls=%fused_computation.3 | convolution fusion | flops 270532608 | bytes 6356992 | tf_op jit(solution)/shard_map/erxij,kj->erxik/dot_general | solution.py:44
  70.3 1.3 %slice_bitcast_fusion.3 = (bf16[1,2,2,2,128,128]{5,4,3,2,1,0:T(8,128)(2,1)S(1)}, bf16[1,2,2,2,128,128]{5,4,3,2,1,0:T(8,128)(2,1)S(1)}, bf16[1,2,2,2,128,128]{5,4...) fusion(bf16[2,8,2,128,128]{4,3,2,1,0:T(8,128)(2,1)} %add_convert_fusion), kind=kLoop, calls=%fused_computation.62 | loop fusion | bytes 2097152 | tf_op jit(solution)/shard_map/stack | solution.py:57
  71.5 0.1 pad_maximum_fusion.1
  71.7 17.1 %all_to_all.5 = bf16[4,2,2,2,128,128]{5,4,3,2,1,0:T(8,128)(2,1)S(1)} all-to-all(bf16[4,2,2,2,128,128]{5,4,3,2,1,0:T(8,128)(2,1)S(1)} %pad_maximum_fusion.1), channel_id=1, replica_groups=mesh['win'=8,'atom'=4] {'atom'}, dimensions={0} | all-to-all | bytes 2097152 | tf_op jit(solution)/shard_map/all_to_all | solution.py:56
  88.7 1.0 %copy.31 = bf16[8,2,2,128,128]{4,3,2,1,0:T(8,128)(2,1)} copy(bf16[8,2,2,128,128]{4,3,2,1,0:T(8,128)(2,1)S(1)} %bitcast.107) | data formatting | bytes 2097152
  (12 shorter events, 0.0 us)
Async XLA Ops:
  0.0 1.7 %copy-start = (bf16[2,8,2,128,128]{4,3,2,1,0:T(8,128)(2,1)S(1)}, bf16[2,8,2,128,128]{4,3,2,1,0:T(8,128)(2,1)}, u32[]{:S(2)}) copy-start(bf16[2,8,2,128,128]{4,3,2,1,0:T(8,128)(2,1)} %param.8) | copy-start | bytes 3145732
  0.0 1.9 %copy-start.1 = (bf16[2,8,2,128,128]{4,3,2,1,0:T(8,128)(2,1)S(1)}, bf16[2,8,2,128,128]{4,3,2,1,0:T(8,128)(2,1)}, u32[]{:S(2)}) copy-start(bf16[2,8,2,128,128]{4,3,2,1,0:T(8,128)(2,1)} %param.9) | copy-start | bytes 3145732
  4.2 7.8 %copy-start.3 = (s32[8,3]{0,1:T(4,128)S(1)}, s32[8,3]{0,1:T(4,128)}, u32[]{:S(2)}) copy-start(s32[8,3]{0,1:T(4,128)} %param.12) | copy-start | bytes 292
  4.2 7.9 %copy-start.4 = (f32[3]{0:T(128)S(1)}, f32[3]{0:T(128)}, u32[]{:S(2)}) copy-start(f32[3]{0:T(128)} %param.11) | copy-start | bytes 40
  4.2 7.9 %copy-start.5 = (s32[3]{0:T(128)S(1)}, s32[3]{0:T(128)}, u32[]{:S(2)}) copy-start(s32[3]{0:T(128)} %param.10) | copy-start | bytes 40
  4.8 49.8 %collective-permute-start.2 = (bf16[2,8,2,128,128]{4,3,1,0,2:T(8,128)(2,1)S(1)}, bf16[2,8,2,128,128]{4,3,1,0,2:T(8,128)(2,1)S(1)}, u32[]{:S(2)}, u32[]{:S(2)}) collective-permute-start(bf16[2,8,2,128,128]{4,3,1,0,2:T(8,128)(2,1)S(1)} %pad_maximum_fusion), channel_id=1, source_target_pairs={{0,16},{4,20},{8,24},{12,28},{16,0},{20,4},{24,8},{28,12},{1,17},{... | collective-permute-start | bytes 3145736 | tf_op jit(solution)/shard_map/ppermute | solution.py:10
  9.0 45.9 %collective-permute-start.1 = (bf16[2,8,2,128,128]{4,3,1,0,2:T(8,128)(2,1)S(1)}, bf16[2,8,2,128,128]{4,3,1,0,2:T(8,128)(2,1)S(1)}, u32[]{:S(2)}, u32[]{:S(2)}) collective-permute-start(bf16[2,8,2,128,128]{4,3,1,0,2:T(8,128)(2,1)S(1)} %pad_maximum_fusion), channel_id=1, source_target_pairs={{0,8},{4,12},{8,0},{12,4},{16,24},{20,28},{24,16},{28,20},{1,9},{5... | collective-permute-start | bytes 3145736 | tf_op jit(solution)/shard_map/ppermute | solution.py:10
  10.5 44.4 %collective-permute-start = (bf16[2,8,2,128,128]{4,3,1,0,2:T(8,128)(2,1)S(1)}, bf16[2,8,2,128,128]{4,3,1,0,2:T(8,128)(2,1)S(1)}, u32[]{:S(2)}, u32[]{:S(2)}) collective-permute-start(bf16[2,8,2,128,128]{4,3,1,0,2:T(8,128)(2,1)S(1)} %pad_maximum_fusion), channel_id=1, source_target_pairs={{0,4},{4,0},{8,12},{12,8},{16,20},{20,16},{24,28},{28,24},{1,5},{5... | collective-permute-start | bytes 3145736 | tf_op jit(solution)/shard_map/ppermute | solution.py:10
  60.5 1.2 %copy-start.2 = (bf16[3,128,128]{2,1,0:T(8,128)(2,1)S(1)}, bf16[3,128,128]{2,1,0:T(8,128)(2,1)}, u32[]{:S(2)}) copy-start(bf16[3,128,128]{2,1,0:T(8,128)(2,1)} %param.13) | copy-start | bytes 294916
